TPU v7x, 256 devices: a whole 4x4x8 slice. The times are simulated.
256 devices in a mesh: half: 2 (over core), rows: 128 (over y, x, z).
Axes of the slice: x: 4, y: 4, z: 8, core: 2. Of those that a mesh axis runs over, the one named last changes fastest.
Arguments:
- factors: float32 [2, 131072, 256], P('half', 'rows'), may hold values from -8 to 8
- coefficients: float32 [256, 256], replicated, may hold values from -1 to 9
- density: float32 [131072], P('rows'), may hold values from 0.25 to 4
Outputs:
- new_factors: float32 [2, 131072, 256], P('half', 'rows')
- new_coefficients: float32 [256, 256], P('half')
All inputs are finite; a program needn't handle non-finite values.
Results may differ from a plain program's by a relative error of at most 0.0001.
Values sent between devices are 32-bit elements; how exact they have to be, the bound alone decides.
No kernel may reach another device: no remote copies, remote signals or barrier semaphores. Data moves between devices by JAX's collectives and lax.ppermute only.
A program may use at most 128 MiB of HBM per device.

v0:
```python
import functools

import jax
import jax.numpy as jnp
from jax import lax
from jax.experimental import pallas as pl
from jax.experimental.pallas import tpu as pltpu
from jax.sharding import Mesh
from jax.sharding import PartitionSpec as P

NZ = 32
VGRID = 64
R = 256
H = R // 2
AXES = ("y", "x", "zh", "zl")
PLANE = ("y", "x", "zl")
CELLS = ("half", "y", "x", "zh", "zl")

time_step = 0.2
relax_time = 0.5
KEEP = 1.0 - time_step / relax_time
GAIN = time_step / relax_time


def dot(a, b, ca=1, cb=0):
    return lax.dot_general(
        a,
        b,
        (((ca,), (cb,)), ((), ())),
        precision=lax.Precision.HIGHEST,
        preferred_element_type=jnp.float32,
    )


def split(x):
    high = x.astype(jnp.bfloat16)
    return high, (x - high.astype(jnp.float32)).astype(jnp.bfloat16)


def dot3(a, b, ca=1, cb=0):
    def part(x, y):
        return lax.dot_general(
            x, y, (((ca,), (cb,)), ((), ())), preferred_element_type=jnp.float32
        )

    return part(a[0], b[0]) + (part(a[0], b[1]) + part(a[1], b[0]))


def plane_scatter(x):
    parts = x.reshape(lax.axis_size(PLANE), -1, x.shape[1])
    return lax.all_to_all(parts, PLANE, 0, 0, tiled=True).sum(axis=0)


def plane_gather(part):
    size = lax.axis_size(PLANE)
    parts = lax.all_to_all(
        jnp.broadcast_to(part[None], (size, *part.shape)), PLANE, 0, 0, tiled=True
    )
    return parts.reshape(size * part.shape[0], part.shape[1])


def line_total(x):
    size = lax.axis_size("zh")
    step = 1
    while step < size:
        x = x + lax.ppermute(x, "zh", [(i, i ^ step) for i in range(size)])
        step *= 2
    return x


def swap_halves(x):
    return lax.ppermute(x, "half", [(0, 1), (1, 0)])


def to_neighbour(x, distance):
    count = lax.axis_size(AXES)
    return lax.ppermute(x, CELLS, [(i, (i + distance) % count) for i in range(count)])


def whole(count):
    return [pl.BlockSpec(memory_space=pltpu.VMEM)] * count


def kernel_call(body, out, arrays, meta, scratch=()):
    outs = out if isinstance(out, list) else [out]
    results = pl.pallas_call(
        body,
        out_shape=[jax.ShapeDtypeStruct(shape, jnp.float32) for shape in outs],
        in_specs=[pl.BlockSpec(memory_space=pltpu.SMEM)] + whole(len(arrays)),
        out_specs=whole(len(outs)),
        scratch_shapes=list(scratch),
    )(meta, *arrays)
    return results if isinstance(out, list) else results[0]


B = 64


def block_inverse(d, out_ref, spread):
    rows = lax.broadcasted_iota(jnp.int32, (B, B), 0)
    cols = lax.broadcasted_iota(jnp.int32, (B, B), 1)
    eye = jnp.where(rows == cols, 1.0, 0.0).astype(jnp.float32)
    wide = jnp.concatenate([d, eye], axis=1)
    count = B // 8
    blk = [wide[8 * i : 8 * i + 8, :] for i in range(count)]
    sub = lax.broadcasted_iota(jnp.int32, (8, 2 * B), 0)

    def lane(v, j):
        return jnp.broadcast_to(v[:, j : j + 1], (8, 2 * B))

    def row(p, k, s):
        return spread[p, k, pl.ds(s, 8, stride=0), :]

    for p in range(count):
        cols_of = [[lane(blk[i], 8 * p + k) for k in range(8)] for i in range(p, count)]
        for k in range(8):
            spread[p, k, :, :] = cols_of[0][k]
        spread[p, 8, :, :] = blk[p]
        piv = {(a, b): row(p, b, a) for a in range(8) for b in range(a, 8)}
        r = [row(p, 8, a) for a in range(8)]
        done = blk[p]
        inv = {}
        for a in range(0, 8, 2):
            d00, d01, d11 = piv[a, a], piv[a, a + 1], piv[a + 1, a + 1]
            inv[a] = 1.0 / (d00 * d11 - d01 * d01)
            ratio = d01 / d00
            done = jnp.where(sub == a, r[a] * (1.0 / jnp.sqrt(d00)), done)
            last = (r[a + 1] - ratio * r[a]) * (1.0 / jnp.sqrt(d11 - ratio * d01))
            done = jnp.where(sub == a + 1, last, done)
            for b in range(a + 2, 8):
                e0, e1 = piv[a, b], piv[a + 1, b]
                t0 = (d11 * e0 - d01 * e1) * inv[a]
                t1 = (d00 * e1 - d01 * e0) * inv[a]
                for c in range(b, 8):
                    piv[b, c] = piv[b, c] - (t0 * piv[a, c] + t1 * piv[a + 1, c])
                r[b] = r[b] - (t0 * r[a] + t1 * r[a + 1])
        out_ref[8 * p : 8 * p + 8, :] = done[:, B:]
        if p + 1 < count:
            w = [None] * 8
            for a in (6, 4, 2, 0):
                y0, y1 = r[a], r[a + 1]
                for b in range(7, a + 1, -1):
                    y0 = y0 - piv[a, b] * w[b]
                    y1 = y1 - piv[a + 1, b] * w[b]
                d00, d01, d11 = piv[a, a], piv[a, a + 1], piv[a + 1, a + 1]
                w[a] = (d11 * y0 - d01 * y1) * inv[a]
                w[a + 1] = (d00 * y1 - d01 * y0) * inv[a]
            for i in range(p + 1, count):
                c = cols_of[i - p]
                even = (c[0] * w[0] + c[2] * w[2]) + (c[4] * w[4] + c[6] * w[6])
                odd = (c[1] * w[1] + c[3] * w[3]) + (c[5] * w[5] + c[7] * w[7])
                blk[i] = blk[i] - (even + odd)


def inverse_factor_body(meta, sums_ref, out_ref, work, small, spread):
    rows = lax.broadcasted_iota(jnp.int32, (R, R), 0)
    cols = lax.broadcasted_iota(jnp.int32, (R, R), 1)
    work[:H, :] = sums_ref[:H, :]
    work[H:, :H] = sums_ref[:H, H:].T
    work[H:, H:] = sums_ref[H:R, H:]
    g = work[...]
    diag = jnp.where(rows == cols, g, 0.0)
    across = 1.0 / jnp.sqrt(jnp.sum(diag, axis=0, keepdims=True))
    down = 1.0 / jnp.sqrt(jnp.sum(diag, axis=1, keepdims=True))
    work[...] = g * across * down
    for k in range(R // B):
        lo, hi = k * B, (k + 1) * B
        block_inverse(work[lo:hi, lo:hi], small, spread)
        ik = small[...]
        left = dot(ik, work[lo:hi, :])
        ccols = lax.broadcasted_iota(jnp.int32, (B, R), 1)
        wide = jnp.concatenate([ik] * (R // B), axis=1)
        panel = jnp.where((ccols >= lo) & (ccols < hi), wide, left)
        work[lo:hi, :] = panel
        if hi < R:
            at = hi // 128 * 128
            update = dot(left[:, at:], panel, 0, 0)
            below = work[hi:, :]
            bcols = lax.broadcasted_iota(jnp.int32, (R - hi, R), 1)
            below = jnp.where((bcols >= lo) & (bcols < hi), 0.0, below)
            work[hi:, :] = below - update[hi - at :, :]
    out_ref[...] = jnp.where(rows >= cols, work[...], 0.0) * across


def upper_mask():
    return lax.broadcasted_iota(jnp.int32, (R, R), 0) <= lax.broadcasted_iota(jnp.int32, (R, R), 1)


def diagonal_mask():
    return lax.broadcasted_iota(jnp.int32, (R, R), 0) == lax.broadcasted_iota(jnp.int32, (R, R), 1)


def shifted_y(x, forward):
    if forward:
        return jnp.concatenate([x[NZ:], x[:NZ]], axis=0)
    return jnp.concatenate([x[-NZ:], x[:-NZ]], axis=0)


def shifted_z(x, forward):
    count = x.shape[0]
    place = lax.broadcasted_iota(jnp.int32, x.shape, 0) & (NZ - 1)
    if forward:
        return jnp.where(
            place == NZ - 1, pltpu.roll(x, NZ - 1, 0), pltpu.roll(x, count - 1, 0)
        )
    return jnp.where(place == 0, pltpu.roll(x, count - NZ + 1, 0), pltpu.roll(x, 1, 0))


def grid_speeds(meta, count, width):
    start = meta[1]
    row = lax.broadcasted_iota(jnp.int32, (count, width), 0)
    third = (row & (NZ - 1)).astype(jnp.float32)
    second = ((start // NZ) % VGRID + row // NZ).astype(jnp.float32)
    first = (start // (NZ * VGRID)).astype(jnp.float32)
    v0 = -1.0 + (2.0 * first + 1.0) / VGRID
    v1 = -1.0 + (2.0 * second + 1.0) / VGRID
    v2 = -1.0 + (2.0 * third + 1.0) / NZ
    maxwell = jnp.exp(-2.0 * (v0 * v0 + v1 * v1 + v2 * v2))
    return v0, v1, v2, maxwell


def first_sign(meta):
    return meta[1] // (NZ * VGRID) >= VGRID // 2


def second_sign(meta):
    return (meta[1] // NZ) % VGRID >= VGRID // 2


def unpack_speed(packed, diag):
    upper, diagonal = upper_mask(), diagonal_mask()
    flipped = packed.T
    plus = jnp.where(upper, packed, flipped)
    minus = jnp.where(diagonal, diag, jnp.where(upper, flipped, packed))
    return plus, minus


def put_speed_sums(meta, f, turned, gram, scale, put_matrix, put_vector):
    upper, diagonal = upper_mask(), diagonal_mask()
    v0, v1, v2, maxwell = grid_speeds(meta, f.shape[0], R)

    def one_sign(d, value, positive):
        low = jnp.where(upper, 0.0, value)
        high = jnp.where(upper, value, 0.0)
        put_matrix(d, jnp.where(positive, high, low))
        diag = jnp.where(diagonal, value, 0.0).sum(axis=0, keepdims=True)
        put_vector(d + 1, jnp.where(positive, 0.0, diag))

    one_sign(0, v0 * gram, first_sign(meta))
    one_sign(1, dot3(turned, split(v1 * f)) * scale, second_sign(meta))
    plus = dot3(turned, split(jnp.maximum(v2, 0.0) * f)) * scale
    minus = dot3(turned, split(jnp.minimum(v2, 0.0) * f)) * scale
    put_matrix(2, jnp.where(upper, plus, minus))
    put_vector(3, jnp.where(diagonal, minus, 0.0).sum(axis=0, keepdims=True))
    put_vector(0, (f * maxwell).sum(axis=0, keepdims=True) * scale)


def first_body(total, meta, f_ref, density_ref, out_ref):
    scale = 1.0 / total
    out_ref[3 * R :, :] = jnp.zeros((R, R), jnp.float32)

    def put_vector(k, value):
        out_ref[3 * R + k : 3 * R + k + 1, :] = value

    def put_matrix(d, value):
        out_ref[d * R : (d + 1) * R, :] = value

    f = f_ref[...]
    turned = split(f.T)

    @pl.when(meta[0] == 0)
    def _():
        put_matrix(0, jnp.zeros((R, R), jnp.float32))
        put_matrix(1, dot3(turned, split(shifted_y(f, True) - f)) * scale)
        put_matrix(2, dot3(turned, split(shifted_z(f, True) - f)) * scale)
        put_vector(0, (f * density_ref[...]).sum(axis=0, keepdims=True) * scale)

    @pl.when(meta[0] == 1)
    def _():
        gram = dot3(turned, split(f)) * scale
        put_speed_sums(meta, f, turned, gram, scale, put_matrix, put_vector)


def across_body(at, total, pairs, meta, *refs):
    *planes, sums_ref, out_ref, block, sem = refs
    del sums_ref

    @pl.when(meta[0] == 0)
    def _():
        left, right = pairs(*planes)
        block[...] = dot3(split(left.T), split(right - left)) * (1.0 / total)
        copy = pltpu.make_async_copy(block, out_ref.at[pl.ds(at, R), :], sem)
        copy.start()
        copy.wait()


def add_across(at, total, pairs, planes, sums, meta):
    return pl.pallas_call(
        functools.partial(across_body, at, total, pairs),
        out_shape=jax.ShapeDtypeStruct(sums.shape, jnp.float32),
        in_specs=[pl.BlockSpec(memory_space=pltpu.SMEM)]
        + whole(len(planes))
        + [pl.BlockSpec(memory_space=pl.ANY)],
        out_specs=pl.BlockSpec(memory_space=pl.ANY),
        scratch_shapes=[pltpu.VMEM((R, R), jnp.float32), pltpu.SemaphoreType.DMA(())],
        input_output_aliases={len(planes) + 1: 0},
        name="across",
    )(meta, *planes, sums)


def with_plane_before(f_ref, previous_low_ref, previous_high_ref):
    return jnp.concatenate([previous_low_ref[...], previous_high_ref[...]], axis=0), f_ref[...]


def with_half_planes(low_ref, high_ref, after_low_ref, before_high_ref):
    left = jnp.concatenate([low_ref[...], before_high_ref[...]], axis=0)
    return left, jnp.concatenate([after_low_ref[...], high_ref[...]], axis=0)


def next_body(
    meta,
    f_ref,
    following_ref,
    previous_low_ref,
    previous_high_ref,
    theirs_ref,
    s_ref,
    density_ref,
    low_ref,
    high_ref,
):
    half = low_ref.shape[0]

    def put(value):
        low_ref[...] = value[:half, :]
        high_ref[...] = value[half:, :]

    def vector(k):
        return theirs_ref[3 * R + k : 3 * R + k + 1, :]

    def matrix(d):
        return theirs_ref[d * R : (d + 1) * R, :]

    @pl.when(meta[0] == 0)
    def _():
        f = f_ref[...]
        following = following_ref[...]
        previous = jnp.concatenate([previous_low_ref[...], previous_high_ref[...]], axis=0)
        s = split(s_ref[...])
        out = dot3(split(f), split(KEEP * s_ref[...])) + GAIN * (density_ref[...] * vector(0))
        for d in range(3):
            plus, minus = unpack_speed(matrix(d), vector(d + 1))
            back = (previous, shifted_y(f, False), shifted_z(f, False))[d]
            ahead = (following, shifted_y(f, True), shifted_z(f, True))[d]
            change = dot3(split(f - back), split(dot3(s, split(plus))))
            change = change + dot3(split(ahead - f), split(dot3(s, split(minus))))
            out = out - time_step * change
        put(out)

    @pl.when(meta[0] == 1)
    def _():
        v0, v1, v2, maxwell = grid_speeds(meta, f_ref.shape[0], R)
        l = dot3(split(f_ref[...]), split(s_ref[...]), 1, 1)
        parts = split(l)
        out = KEEP * l + GAIN * (maxwell * vector(0))
        for d, v, positive in ((0, v0, first_sign(meta)), (1, v1, second_sign(meta))):
            e = matrix(d)
            out = out - time_step * (v * dot3(parts, split(jnp.where(positive, -e, e.T))))
        e = split(matrix(2))
        out = out + time_step * (jnp.maximum(v2, 0.0) * dot3(parts, e))
        put(out - time_step * (jnp.minimum(v2, 0.0) * dot3(parts, e, 1, 1)))


def second_body(total, meta, low_ref, high_ref, f_ref, density_ref, out_ref, k_ref):
    scale = 1.0 / total
    k = jnp.concatenate([low_ref[...], high_ref[...]], axis=0)
    k_ref[...] = k
    straight = k.T
    gram = dot(straight, k) * scale
    turned = split(straight)
    out_ref[:H, :] = gram[:H, :]
    out_ref[H:R, :H] = jnp.zeros((H, H), jnp.float32)
    out_ref[H:R, H:] = gram[H:, H:]

    def put_matrix(d, value):
        out_ref[(2 + d) * R : (3 + d) * R, :] = value

    def put_vector(i, value):
        out_ref[H + 2 * i : H + 2 * i + 1, :H] = value[:, :H]
        out_ref[H + 2 * i + 1 : H + 2 * i + 2, :H] = value[:, H:]

    put_matrix(-1, dot3(turned, split(f_ref[...])) * scale)

    @pl.when(meta[0] == 0)
    def _():
        put_matrix(0, jnp.zeros((R, R), jnp.float32))
        put_matrix(1, dot3(turned, split(shifted_y(k, True) - k)) * scale)
        put_matrix(2, dot3(turned, split(shifted_z(k, True) - k)) * scale)
        put_vector(0, (k * density_ref[...]).sum(axis=0, keepdims=True) * scale)

    @pl.when(meta[0] == 1)
    def _():
        put_speed_sums(meta, k, turned, gram, scale, put_matrix, put_vector)


def basis_body(meta, k_ref, inverse_ref, out_ref):
    out_ref[...] = dot(k_ref[...], inverse_ref[...].T)


def coefficient_body(
    meta,
    mine_ref,
    other_ref,
    inverse_ref,
    other_inverse_ref,
    s_ref,
    out_ref,
):
    def work(half, space_ref, speed_ref, pk_ref, pv_ref):
        def vector(ref, k):
            at = H + 2 * k
            return jnp.concatenate([ref[at : at + 1, :H], ref[at + 1 : at + 2, :H]], axis=1)

        pk, pv = pk_ref[...], pv_ref[...]
        rows = pk[half * H : (half + 1) * H, :]
        middle = dot(dot(space_ref[R : 2 * R, :], s_ref[...]), speed_ref[R : 2 * R, :], 1, 1)
        turned = dot(pk, middle)
        z = dot(dot(pk, turned, 0, 0), dot(pv, pv, 0, 0))
        row_parts = split(rows)
        parts = []
        for d in range(3):
            h = split(space_ref[(2 + d) * R : (3 + d) * R, :])
            parts += [dot3(row_parts, h), dot3(row_parts, h, 1, 1)]
        parts = dot3(split(jnp.concatenate(parts, axis=0)), split(z))
        change = jnp.zeros((H, R), jnp.float32)
        for d in range(3):
            packed = speed_ref[(2 + d) * R : (3 + d) * R, :]
            plus, minus = unpack_speed(packed, vector(speed_ref, d + 1))
            change = change + dot3(split(parts[2 * d * H : (2 * d + 1) * H, :]), split(minus))
            change = change - dot3(split(parts[(2 * d + 1) * H : (2 * d + 2) * H, :]), split(plus))
        xb = jnp.sum(rows * vector(space_ref, 0), axis=1, keepdims=True)
        out = KEEP * turned[half * H : (half + 1) * H, :] - time_step * change
        out = out + GAIN * (xb * vector(speed_ref, 0))
        out_ref[...] = dot(out, pv, 1, 1)

    @pl.when(meta[0] == 0)
    def _():
        work(0, mine_ref, other_ref, inverse_ref, other_inverse_ref)

    @pl.when(meta[0] == 1)
    def _():
        work(1, other_ref, mine_ref, other_inverse_ref, inverse_ref)


def step(factors, coefficients, density):
    rows_here = factors.shape[1]
    total = rows_here * lax.axis_size(AXES)
    start = lax.axis_index(AXES) * rows_here
    meta = jnp.stack([lax.axis_index("half"), start]).astype(jnp.int32)
    f = factors[0]
    column = density[:, None]

    half = rows_here // 2
    low, high = f[:half], f[half:]
    previous_high = to_neighbour(high, 1)
    previous_low = to_neighbour(low, 1)
    following = to_neighbour(f, -1)

    sums = kernel_call(functools.partial(first_body, total), (4 * R, R), [f, column], meta)
    sums = add_across(0, total, with_plane_before, [f, previous_low, previous_high], sums, meta)
    theirs = plane_gather(swap_halves(line_total(plane_scatter(sums))))
    low, high = kernel_call(
        next_body,
        [(half, R)] * 2,
        [f, following, previous_low, previous_high, theirs, coefficients, column],
        meta,
    )

    before_high = to_neighbour(high, 1)
    after_low = to_neighbour(low, -1)
    sums, fresh = kernel_call(
        functools.partial(second_body, total),
        [(5 * R, R), (rows_here, R)],
        [low, high, f, column],
        meta,
    )
    sums = add_across(
        2 * R, total, with_half_planes, [low, high, after_low, before_high], sums, meta
    )
    mine = plane_gather(line_total(plane_scatter(sums)))
    other = swap_halves(mine)
    inverse = kernel_call(
        inverse_factor_body,
        (R, R),
        [mine],
        meta,
        [
            pltpu.VMEM((R, R), jnp.float32),
            pltpu.VMEM((B, B), jnp.float32),
            pltpu.VMEM((B // 8, 9, 8, 2 * B), jnp.float32),
        ],
    )
    basis = kernel_call(basis_body, (rows_here, R), [fresh, inverse], meta)
    other_inverse = swap_halves(inverse)
    updated = kernel_call(
        coefficient_body, (H, R), [mine, other, inverse, other_inverse, coefficients], meta
    )
    return (basis[None], updated)


def solution(mesh):
    torus = Mesh(mesh.devices.reshape(mesh.shape["half"], 4, 4, 4, 2), CELLS)
    return jax.shard_map(
        step,
        mesh=torus,
        in_specs=(P("half", AXES, None), P(), P(AXES)),
        out_specs=(P("half", AXES, None), P("half", None)),
        check_vma=False,
    )
```

profile of v0, /device:TPU:1, one launch (start us, length us, event | category | flops | bytes accessed | tf_op | source)
XLA Modules:
  0.0 216.4 jit_solution(11571150719871740285)
XLA Ops:
  0.6 0.0 copy-start.10
  0.6 1.3 slice_bitcast_fusion
  1.9 0.7 collective-permute-start.1
  2.6 0.7 collective-permute-start.2
  3.3 0.0 copy-done.10
  3.3 1.0 copy.7.density_ref
  4.4 0.6 pad_add_fusion.meta
  5.0 4.8 %shard_map.50.refs_3_ = f32[1024,256]{1,0:T(8,128)} custom-call(s32[2]{0:T(128)} %pad_add_fusion.meta, f32[1024,256]{1,0:T(8,128)} %bitcast.13, f32[1024,1]{1,0:T(8,128)} %copy.7.density_ref), custom_call_target="tpu_custom_call" | custom-call | tf_op jit(solution)/shard_map/pallas_call | solution.py:86
  9.8 0.0 collective-permute-done.1.refs_1_.previous_low_ref
  9.8 0.0 copy-start.3
  9.8 0.0 collective-permute-done.2.refs_2_.previous_high_ref
  9.8 0.8 copy-done.3
  10.6 0.0 copy-start.4
  10.6 0.8 copy-done.4
  11.4 1.5 across.2
  12.9 21.8 %all_to_all.20 = f32[32,32,256]{2,1,0:T(8,128)S(1)} all-to-all(f32[32,32,256]{2,1,0:T(8,128)} %bitcast.21), channel_id=1, replica_groups=mesh['half'=2,'y'=4,'x'=4,'zh'=4,'zl'=2] {'y','x','zl'}, dimensions={0} | all-to-all | bytes 2097152 | tf_op jit(solution)/shard_map/all_to_all | solution.py:51
  34.7 0.1 reduce_sum.18
  34.7 3.1 %collective-permute-start.3 = (f32[32,256]{1,0:T(8,128)S(1)}, f32[32,256]{1,0:T(8,128)S(1)}, u32[]{:S(2)}, u32[]{:S(2)}) collective-permute-start(f32[32,256]{1,0:T(8,128)S(1)} %reduce_sum.18), channel_id=1, source_target_pairs={{0,2},{2,0},{4,6},{6,4},{1,3},{3,1},{5,7},{7,5},{8,10},{10,8},{12,... | collective-permute-start | bytes 98312 | tf_op jit(solution)/shard_map/ppermute | solution.py:66
  37.8 1.6 collective-permute-done.3
  39.5 5.7 %collective-permute-start.4 = (f32[32,256]{1,0:T(8,128)S(1)}, f32[32,256]{1,0:T(8,128)S(1)}, u32[]{:S(2)}, u32[]{:S(2)}) collective-permute-start(f32[32,256]{1,0:T(8,128)S(1)} %add.24), channel_id=1, source_target_pairs={{0,4},{2,6},{4,0},{6,2},{1,5},{3,7},{5,1},{7,3},{8,12},{10,14},{12... | collective-permute-start | bytes 98312 | tf_op jit(solution)/shard_map/ppermute | solution.py:66
  45.1 1.9 collective-permute-done.4
  47.1 17.9 %collective-permute-start.5 = (f32[32,256]{1,0:T(8,128)S(1)}, f32[32,256]{1,0:T(8,128)S(1)}, u32[]{:S(2)}, u32[]{:S(2)}) collective-permute-start(f32[32,256]{1,0:T(8,128)S(1)} %add.25), channel_id=1, source_target_pairs={{0,128},{128,0},{1,129},{129,1},{2,130},{130,2},{3,131},{131,3},{4... | collective-permute-start | bytes 98312 | tf_op jit(solution)/shard_map/ppermute | solution.py:72
  64.9 0.9 collective-permute-done.5
  65.8 1.1 broadcast_in_dim.9
  66.9 0.0 copy-start
  66.9 4.1 %all-to-all-start.1 = ((f32[32,32,256]{2,1,0:T(8,128)}), f32[32,32,256]{2,1,0:T(8,128)S(1)}, u32[]{:S(2)}, u32[]{:S(2)}) async-start(f32[32,32,256]{2,1,0:T(8,128)} %broadcast_in_dim.9), calls=%async_computation.1 | async-start | bytes 2097152 | tf_op jit(solution)/shard_map/all_to_all | solution.py:56
  71.0 0.0 copy-done
  71.0 0.7 collective-permute-start
  71.7 0.0 collective-permute-done.following_ref
  71.8 0.0 copy-start.6
  71.8 16.5 %all-to-all-done.1 = f32[32,32,256]{2,1,0:T(8,128)S(1)} async-done(((f32[32,32,256]{2,1,0:T(8,128)}), f32[32,32,256]{2,1,0:T(8,128)S(1)}, u32[]{:S(2)}, u32[]{:S(2)}) %all-to-all-start.1) | async-done | bytes 1048608 | tf_op jit(solution)/shard_map/all_to_all | solution.py:56
  88.3 0.0 copy-start.2
  88.3 0.0 copy-done.6
  88.3 1.0 copy-done.2
  89.3 6.7 %shard_map.51 = (f32[512,256]{1,0:T(8,128)}, f32[512,256]{1,0:T(8,128)}) custom-call(s32[2]{0:T(128)} %pad_add_fusion.meta, f32[1024,256]{1,0:T(8,128)} %bitcast.15, f32[1024,256]{1,0:T(8,128)} %copy-done.6, f32[512,256]{1,0:T(8,128)} %copy-done.3, f32[512,256]{1,0:T(8,128)} %copy-done.4, f32[1024,256]{1,0:T(8,128)} %bitcast.23, f32[256,256]{1,0:T(8,128)} %s_ref.3, ...), custom_call_target="tpu_custom_call" | custom-call | tf_op jit(solution)/shard_map/pallas_call | solution.py:86
  96.0 0.7 collective-permute-start.6
  96.6 0.7 collective-permute-start.7
  97.3 6.6 %shard_map.52 = (f32[1280,256]{1,0:T(8,128)}, f32[1024,256]{1,0:T(8,128)}) custom-call(s32[2]{0:T(128)} %pad_add_fusion.meta, f32[512,256]{1,0:T(8,128)} %get-tuple-element.6.low_ref.refs_0_, f32[512,256]{1,0:T(8,128)} %get-tuple-element.7.high_ref.refs_1_, f32[1024,256]{1,0:T(8,128)} %bitcast.16, f32[1024,1]{1,0:T(8,128)} %copy.7.density_ref), custom_call_target="tpu_custom_call" | custom-call | tf_op jit(solution)/shard_map/pallas_call | solution.py:86
  103.9 0.0 collective-permute-done.6.refs_2_
  103.9 0.0 collective-permute-done.7.refs_3_
  103.9 0.0 copy-start.8
  103.9 0.8 copy-done.7
  104.7 0.2 copy-done.8
  104.9 1.5 across.3
  106.4 24.2 %all_to_all.21 = f32[32,40,256]{2,1,0:T(8,128)S(1)} all-to-all(f32[32,40,256]{2,1,0:T(8,128)} %bitcast.22), channel_id=1, replica_groups=mesh['half'=2,'y'=4,'x'=4,'zh'=4,'zl'=2] {'y','x','zl'}, dimensions={0} | all-to-all | bytes 2621440 | tf_op jit(solution)/shard_map/all_to_all | solution.py:51
  130.6 0.1 reduce_sum.19
  130.7 0.1 collective-permute-start.8
  130.8 3.7 %collective-permute-done.8 = f32[40,256]{1,0:T(8,128)S(1)} collective-permute-done((f32[40,256]{1,0:T(8,128)S(1)}, f32[40,256]{1,0:T(8,128)S(1)}, u32[]{:S(2)}, u32[]{:S(2)}) %collective-permute-start.8) | collective-permute-done | bytes 40992 | tf_op jit(solution)/shard_map/ppermute | solution.py:66
  134.6 5.6 %collective-permute-start.9 = (f32[40,256]{1,0:T(8,128)S(1)}, f32[40,256]{1,0:T(8,128)S(1)}, u32[]{:S(2)}, u32[]{:S(2)}) collective-permute-start(f32[40,256]{1,0:T(8,128)S(1)} %add.26), channel_id=1, source_target_pairs={{0,4},{2,6},{4,0},{6,2},{1,5},{3,7},{5,1},{7,3},{8,12},{10,14},{12... | collective-permute-start | bytes 122888 | tf_op jit(solution)/shard_map/ppermute | solution.py:66
  140.1 1.8 collective-permute-done.9
  142.0 0.1 broadcast_in_dim.20
  142.1 19.3 %all_to_all.22 = f32[32,40,256]{2,1,0:T(8,128)S(1)} all-to-all(f32[32,40,256]{2,1,0:T(8,128)S(1)} %broadcast_in_dim.20), channel_id=1, replica_groups=mesh['half'=2,'y'=4,'x'=4,'zh'=4,'zl'=2] {'y','x','zl'}, dimensions={0} | all-to-all | bytes 2621440 | tf_op jit(solution)/shard_map/all_to_all | solution.py:56
  161.4 0.0 copy-start.1
  161.4 30.0 %collective-permute-start.10 = (f32[1280,256]{1,0:T(8,128)S(1)}, f32[1280,256]{1,0:T(8,128)S(1)}, u32[]{:S(2)}, u32[]{:S(2)}) collective-permute-start(f32[1280,256]{1,0:T(8,128)S(1)} %bitcast.18), channel_id=1, source_target_pairs={{0,128},{128,0},{1,129},{129,1},{2,130},{130,2},{3,131},{131,3},{4... | collective-permute-start | bytes 3932168 | tf_op jit(solution)/shard_map/ppermute | solution.py:72
  191.4 0.0 copy-done.1
  191.4 11.7 %shard_map.53.inverse_ref = f32[256,256]{1,0:T(8,128)} custom-call(s32[2]{0:T(128)} %pad_add_fusion.meta, f32[1280,256]{1,0:T(8,128)} %bitcast.19), custom_call_target="tpu_custom_call" | custom-call | tf_op jit(solution)/shard_map/pallas_call | solution.py:86
  203.1 1.1 collective-permute-start.11
  204.1 3.3 %shard_map.54 = f32[1024,256]{1,0:T(8,128)} custom-call(s32[2]{0:T(128)} %pad_add_fusion.meta, f32[1024,256]{1,0:T(8,128)} %get-tuple-element.8.k_ref, f32[256,256]{1,0:T(8,128)} %shard_map.53.inverse_ref), custom_call_target="tpu_custom_call" | custom-call | tf_op jit(solution)/shard_map/pallas_call | solution.py:86
  207.4 0.0 collective-permute-done.11.other_inverse_ref
  207.4 0.0 copy-start.9
  207.4 0.0 collective-permute-done.10.other_ref
  207.4 0.7 copy-done.9
  208.1 1.1 copy-done.5
  209.2 7.2 %shard_map.55 = f32[128,256]{1,0:T(8,128)} custom-call(s32[2]{0:T(128)} %pad_add_fusion.meta, f32[1280,256]{1,0:T(8,128)} %bitcast.20, f32[1280,256]{1,0:T(8,128)} %copy-done.5, f32[256,256]{1,0:T(8,128)} %shard_map.53.inverse_ref, f32[256,256]{1,0:T(8,128)} %copy-done.9, f32[256,256]{1,0:T(8,128)} %s_ref.3), custom_call_target="tpu_custom_call" | custom-call | tf_op jit(solution)/shard_map/pallas_call | solution.py:86
  (6 shorter events, 0.0 us)
Async XLA Ops:
  0.6 2.7 %copy-start.10 = (f32[1024]{0:T(1024)S(1)}, f32[1024]{0:T(1024)}, u32[]{:S(2)}) copy-start(f32[1024]{0:T(1024)} %param.5) | copy-start | bytes 12292
  1.9 7.8 %collective-permute-start.1 = (f32[512,256]{1,0:T(8,128)S(1)}, f32[512,256]{1,0:T(8,128)S(1)}, u32[]{:S(2)}, u32[]{:S(2)}) collective-permute-start(f32[512,256]{1,0:T(8,128)S(1)} %get-tuple-element.11), channel_id=1, source_target_pairs={{0,1},{1,2},{2,3},{3,4},{4,5},{5,6},{6,7},{7,8},{8,9},{9,10},{10,1... | collective-permute-start | bytes 1572872 | tf_op jit(solution)/shard_map/ppermute | solution.py:77
  2.6 7.1 %collective-permute-start.2 = (f32[512,256]{1,0:T(8,128)S(1)}, f32[512,256]{1,0:T(8,128)S(1)}, u32[]{:S(2)}, u32[]{:S(2)}) collective-permute-start(f32[512,256]{1,0:T(8,128)S(1)} %get-tuple-element.10), channel_id=1, source_target_pairs={{0,1},{1,2},{2,3},{3,4},{4,5},{5,6},{6,7},{7,8},{8,9},{9,10},{10,1... | collective-permute-start | bytes 1572872 | tf_op jit(solution)/shard_map/ppermute | solution.py:77
  9.8 0.8 copy-start.3
  10.6 0.8 copy-start.4
  34.7 4.7 %collective-permute-start.3 = (f32[32,256]{1,0:T(8,128)S(1)}, f32[32,256]{1,0:T(8,128)S(1)}, u32[]{:S(2)}, u32[]{:S(2)}) collective-permute-start(f32[32,256]{1,0:T(8,128)S(1)} %reduce_sum.18), channel_id=1, source_target_pairs={{0,2},{2,0},{4,6},{6,4},{1,3},{3,1},{5,7},{7,5},{8,10},{10,8},{12,... | collective-permute-start | bytes 98312 | tf_op jit(solution)/shard_map/ppermute | solution.py:66
  39.5 7.6 %collective-permute-start.4 = (f32[32,256]{1,0:T(8,128)S(1)}, f32[32,256]{1,0:T(8,128)S(1)}, u32[]{:S(2)}, u32[]{:S(2)}) collective-permute-start(f32[32,256]{1,0:T(8,128)S(1)} %add.24), channel_id=1, source_target_pairs={{0,4},{2,6},{4,0},{6,2},{1,5},{3,7},{5,1},{7,3},{8,12},{10,14},{12... | collective-permute-start | bytes 98312 | tf_op jit(solution)/shard_map/ppermute | solution.py:66
  47.1 18.7 %collective-permute-start.5 = (f32[32,256]{1,0:T(8,128)S(1)}, f32[32,256]{1,0:T(8,128)S(1)}, u32[]{:S(2)}, u32[]{:S(2)}) collective-permute-start(f32[32,256]{1,0:T(8,128)S(1)} %add.25), channel_id=1, source_target_pairs={{0,128},{128,0},{1,129},{129,1},{2,130},{130,2},{3,131},{131,3},{4... | collective-permute-start | bytes 98312 | tf_op jit(solution)/shard_map/ppermute | solution.py:72
  66.9 4.1 %copy-start = (f32[1,1024,256]{2,1,0:T(8,128)S(1)}, f32[1,1024,256]{2,1,0:T(8,128)}, u32[]{:S(2)}) copy-start(f32[1,1024,256]{2,1,0:T(8,128)} %param.3) | copy-start | bytes 3145732
  66.9 21.4 %all-to-all-start.1 = ((f32[32,32,256]{2,1,0:T(8,128)}), f32[32,32,256]{2,1,0:T(8,128)S(1)}, u32[]{:S(2)}, u32[]{:S(2)}) async-start(f32[32,32,256]{2,1,0:T(8,128)} %broadcast_in_dim.9), calls=%async_computation.1 | async-start | bytes 2097152 | tf_op jit(solution)/shard_map/all_to_all | solution.py:56
  71.0 0.7 collective-permute-start
  71.8 16.5 %copy-start.6 = (f32[1024,256]{1,0:T(8,128)}, f32[1024,256]{1,0:T(8,128)S(1)}, u32[]{:S(2)}) copy-start(f32[1024,256]{1,0:T(8,128)S(1)} %collective-permute-done.following_ref) | copy-start | bytes 3145732
  88.3 1.0 copy-start.2
  96.0 8.0 %collective-permute-start.6 = (f32[512,256]{1,0:T(8,128)}, f32[512,256]{1,0:T(8,128)S(1)}, u32[]{:S(2)}, u32[]{:S(2)}) collective-permute-start(f32[512,256]{1,0:T(8,128)} %get-tuple-element.6.low_ref.refs_0_), channel_id=1, source_target_pairs={{0,127},{1,0},{2,1},{3,2},{4,3},{5,4},{6,5},{7,6},{8,7},{9,8},{10,... | collective-permute-start | bytes 1572872 | tf_op jit(solution)/shard_map/ppermute | solution.py:77
  96.6 7.3 %collective-permute-start.7 = (f32[512,256]{1,0:T(8,128)}, f32[512,256]{1,0:T(8,128)S(1)}, u32[]{:S(2)}, u32[]{:S(2)}) collective-permute-start(f32[512,256]{1,0:T(8,128)} %get-tuple-element.7.high_ref.refs_1_), channel_id=1, source_target_pairs={{0,1},{1,2},{2,3},{3,4},{4,5},{5,6},{6,7},{7,8},{8,9},{9,10},{10,1... | collective-permute-start | bytes 1572872 | tf_op jit(solution)/shard_map/ppermute | solution.py:77
  103.9 0.8 copy-start.7
  103.9 1.0 copy-start.8
  130.7 3.8 %collective-permute-start.8 = (f32[40,256]{1,0:T(8,128)S(1)}, f32[40,256]{1,0:T(8,128)S(1)}, u32[]{:S(2)}, u32[]{:S(2)}) collective-permute-start(f32[40,256]{1,0:T(8,128)S(1)} %reduce_sum.19), channel_id=1, source_target_pairs={{0,2},{2,0},{4,6},{6,4},{1,3},{3,1},{5,7},{7,5},{8,10},{10,8},{12,... | collective-permute-start | bytes 122888 | tf_op jit(solution)/shard_map/ppermute | solution.py:66
  134.6 7.4 %collective-permute-start.9 = (f32[40,256]{1,0:T(8,128)S(1)}, f32[40,256]{1,0:T(8,128)S(1)}, u32[]{:S(2)}, u32[]{:S(2)}) collective-permute-start(f32[40,256]{1,0:T(8,128)S(1)} %add.26), channel_id=1, source_target_pairs={{0,4},{2,6},{4,0},{6,2},{1,5},{3,7},{5,1},{7,3},{8,12},{10,14},{12... | collective-permute-start | bytes 122888 | tf_op jit(solution)/shard_map/ppermute | solution.py:66
  161.4 30.0 %copy-start.1 = (f32[32,40,256]{2,1,0:T(8,128)}, f32[32,40,256]{2,1,0:T(8,128)S(1)}, u32[]{:S(2)}) copy-start(f32[32,40,256]{2,1,0:T(8,128)S(1)} %all_to_all.22) | copy-start | bytes 3932164
  161.4 46.0 %collective-permute-start.10 = (f32[1280,256]{1,0:T(8,128)S(1)}, f32[1280,256]{1,0:T(8,128)S(1)}, u32[]{:S(2)}, u32[]{:S(2)}) collective-permute-start(f32[1280,256]{1,0:T(8,128)S(1)} %bitcast.18), channel_id=1, source_target_pairs={{0,128},{128,0},{1,129},{129,1},{2,130},{130,2},{3,131},{131,3},{4... | collective-permute-start | bytes 3932168 | tf_op jit(solution)/shard_map/ppermute | solution.py:72
  203.1 4.3 %collective-permute-start.11 = (f32[256,256]{1,0:T(8,128)}, f32[256,256]{1,0:T(8,128)S(1)}, u32[]{:S(2)}, u32[]{:S(2)}) collective-permute-start(f32[256,256]{1,0:T(8,128)} %shard_map.53.inverse_ref), channel_id=1, source_target_pairs={{0,128},{128,0},{1,129},{129,1},{2,130},{130,2},{3,131},{131,3},{4... | collective-permute-start | bytes 786440 | tf_op jit(solution)/shard_map/ppermute | solution.py:72
  207.4 0.7 copy-start.9
  208.1 1.1 copy-start.5
where the time goes:
time: 217 us; the launch traced here: 216 us
  starting transfers between devices  70.9 us (33%)
  blocking collectives  65.3 us (30%)
  Pallas kernels  43.2 us (20%)
  waiting for transfers between devices  26.5 us (12%)
  local copies, waits for them, and re-layouts  8.86 us (4%)
    ppermute x3, starting transfers between devices, swap_halves(): return lax.ppermute(x, 'half', [(0, 1), (1, 0)])  48.9 us
    all_to_all x2, blocking collectives, plane_scatter(): return lax.all_to_all(parts, PLANE, 0, 0, tiled=True).sum(axis=0)  46 us
    pallas_call x6, Pallas kernels, kernel_call(): pl.pallas_call(body, out_shape=[jax.ShapeDtypeStruct(shape, jnp.float32)...  40.2 us
    all_to_all x1, blocking collectives, plane_gather(): lax.all_to_all(jnp.broadcast_to(part[None], (size, *part.shape)), PLANE,...  19.3 us
    all_to_all x1, waiting for transfers between devices, plane_gather(): lax.all_to_all(jnp.broadcast_to(part[None], (size, *part.shape)), PLANE,...  16.5 us
    ppermute x4, starting transfers between devices, line_total(): x = x + lax.ppermute(x, 'zh', [(i, i ^ step) for i in range(size)])  14.4 us
    ppermute x4, waiting for transfers between devices, line_total(): x = x + lax.ppermute(x, 'zh', [(i, i ^ step) for i in range(size)])  9.13 us
    unnamed x22, local copies, waits for them, and re-layouts  5.33 us
  transfers between devices with their start and end apart: 13, of which 6 were waited for; matrix products, arithmetic and copies ran while one was open for 1% of the time, Pallas kernels for 12%

commit v1 on v0

--- a/solution.py
+++ b/solution.py
@@ -12,6 +12,7 @@
 VGRID = 64
 R = 256
 H = R // 2
+VMEM_LIMIT = 20 << 20
 AXES = ("y", "x", "zh", "zl")
 PLANE = ("y", "x", "zl")
 CELLS = ("half", "y", "x", "zh", "zl")
@@ -81,14 +82,16 @@
     return [pl.BlockSpec(memory_space=pltpu.VMEM)] * count
 
 
-def kernel_call(body, out, arrays, meta, scratch=()):
+def kernel_call(body, out, arrays, meta, scratch=(), fetch=False):
     outs = out if isinstance(out, list) else [out]
     results = pl.pallas_call(
         body,
         out_shape=[jax.ShapeDtypeStruct(shape, jnp.float32) for shape in outs],
-        in_specs=[pl.BlockSpec(memory_space=pltpu.SMEM)] + whole(len(arrays)),
+        in_specs=[pl.BlockSpec(memory_space=pltpu.SMEM)]
+        + ([pl.BlockSpec(memory_space=pl.ANY)] * len(arrays) if fetch else whole(len(arrays))),
         out_specs=whole(len(outs)),
         scratch_shapes=list(scratch),
+        compiler_params=pltpu.CompilerParams(vmem_limit_bytes=VMEM_LIMIT),
     )(meta, *arrays)
     return results if isinstance(out, list) else results[0]
 
@@ -152,12 +155,15 @@
                 blk[i] = blk[i] - (even + odd)
 
 
-def inverse_factor_body(meta, sums_ref, out_ref, work, small, spread):
+def inverse_factor_body(meta, sums_ref, out_ref, work, small, spread, gram_ref, sem):
+    copy = pltpu.make_async_copy(sums_ref.at[pl.ds(0, R), :], gram_ref, sem)
+    copy.start()
+    copy.wait()
     rows = lax.broadcasted_iota(jnp.int32, (R, R), 0)
     cols = lax.broadcasted_iota(jnp.int32, (R, R), 1)
-    work[:H, :] = sums_ref[:H, :]
-    work[H:, :H] = sums_ref[:H, H:].T
-    work[H:, H:] = sums_ref[H:R, H:]
+    work[:H, :] = gram_ref[:H, :]
+    work[H:, :H] = gram_ref[:H, H:].T
+    work[H:, H:] = gram_ref[H:R, H:]
     g = work[...]
     diag = jnp.where(rows == cols, g, 0.0)
     across = 1.0 / jnp.sqrt(jnp.sum(diag, axis=0, keepdims=True))
@@ -304,12 +310,13 @@
         out_specs=pl.BlockSpec(memory_space=pl.ANY),
         scratch_shapes=[pltpu.VMEM((R, R), jnp.float32), pltpu.SemaphoreType.DMA(())],
         input_output_aliases={len(planes) + 1: 0},
+        compiler_params=pltpu.CompilerParams(vmem_limit_bytes=VMEM_LIMIT),
         name="across",
     )(meta, *planes, sums)
 
 
-def with_plane_before(f_ref, previous_low_ref, previous_high_ref):
-    return jnp.concatenate([previous_low_ref[...], previous_high_ref[...]], axis=0), f_ref[...]
+def with_plane_before(f_ref, previous_ref):
+    return previous_ref[...], f_ref[...]
 
 
 def with_half_planes(low_ref, high_ref, after_low_ref, before_high_ref):
@@ -321,8 +328,7 @@
     meta,
     f_ref,
     following_ref,
-    previous_low_ref,
-    previous_high_ref,
+    previous_ref,
     theirs_ref,
     s_ref,
     density_ref,
@@ -345,7 +351,7 @@
     def _():
         f = f_ref[...]
         following = following_ref[...]
-        previous = jnp.concatenate([previous_low_ref[...], previous_high_ref[...]], axis=0)
+        previous = previous_ref[...]
         s = split(s_ref[...])
         out = dot3(split(f), split(KEEP * s_ref[...])) + GAIN * (density_ref[...] * vector(0))
         for d in range(3):
@@ -461,19 +467,16 @@
     column = density[:, None]
 
     half = rows_here // 2
-    low, high = f[:half], f[half:]
-    previous_high = to_neighbour(high, 1)
-    previous_low = to_neighbour(low, 1)
+    previous = to_neighbour(f, 1)
     following = to_neighbour(f, -1)
 
     sums = kernel_call(functools.partial(first_body, total), (4 * R, R), [f, column], meta)
-    sums = add_across(0, total, with_plane_before, [f, previous_low, previous_high], sums, meta)
-    theirs = plane_gather(swap_halves(line_total(plane_scatter(sums))))
+    sums = add_across(0, total, with_plane_before, [f, previous], sums, meta)
+    part = swap_halves(line_total(plane_scatter(sums)))
+    part, following = lax.optimization_barrier((part, following))
+    theirs = plane_gather(part)
     low, high = kernel_call(
-        next_body,
-        [(half, R)] * 2,
-        [f, following, previous_low, previous_high, theirs, coefficients, column],
-        meta,
+        next_body, [(half, R)] * 2, [f, following, previous, theirs, coefficients, column], meta
     )
 
     before_high = to_neighbour(high, 1)
@@ -498,7 +501,10 @@
             pltpu.VMEM((R, R), jnp.float32),
             pltpu.VMEM((B, B), jnp.float32),
             pltpu.VMEM((B // 8, 9, 8, 2 * B), jnp.float32),
+            pltpu.VMEM((R, R), jnp.float32),
+            pltpu.SemaphoreType.DMA(()),
         ],
+        fetch=True,
     )
     basis = kernel_call(basis_body, (rows_here, R), [fresh, inverse], meta)
     other_inverse = swap_halves(inverse)

time: 217 us -> 191 us (0.88)
  starting transfers between devices: 70.9 us -> 59.3 us
  Pallas kernels: 43.2 us -> 32.2 us
  local copies, waits for them, and re-layouts: 8.86 us -> 2.33 us
  waiting for transfers between devices: 26.5 us -> 31.9 us
  blocking collectives: 65.3 us -> 61.9 us
    all_to_all x2 -> x1, blocking collectives: 46 us -> 21.3 us  [plane_scatter(): return lax.all_to_all(parts, PLANE, 0, 0, tiled=True).sum(axis=0)]
    all_to_all x1 -> x2, blocking collectives: 19.3 us -> 40.7 us  [plane_gather(): lax.all_to_all(jnp.broadcast_to(part[None], (size, *part.shape)), PLANE,...]
    ppermute x4, starting transfers between devices: 14.4 us -> 4.39 us  [line_total(): x = x + lax.ppermute(x, 'zh', [(i, i ^ step) for i in range(size)])]
    pallas_call x6, Pallas kernels: 40.2 us -> 31.1 us  [kernel_call(): pl.pallas_call(body, out_shape=[jax.ShapeDtypeStruct(shape, jnp.float32)...]
    ppermute x4, waiting for transfers between devices: 9.13 us -> 17.6 us  [line_total(): x = x + lax.ppermute(x, 'zh', [(i, i ^ step) for i in range(size)])]
    ppermute x3, starting transfers between devices: 48.9 us -> 41.6 us  [swap_halves(): return lax.ppermute(x, 'half', [(0, 1), (1, 0)])]
    all_to_all x1, starting transfers between devices: 4.06 us -> 9.49 us  [plane_scatter(): return lax.all_to_all(parts, PLANE, 0, 0, tiled=True).sum(axis=0)]
    unnamed x22 -> x6, local copies, waits for them, and re-layouts: 5.33 us -> 1.24 us
  transfers between devices with their start and end apart: 13 -> 12, of which waited for: 6 -> 6; matrix products, arithmetic and copies ran while one was open for 1% -> 1% of each run, Pallas kernels for 12% -> 11%
where the time goes in v1:
time: 191 us; the launch traced here: 190 us
  blocking collectives  61.9 us (32%)
  starting transfers between devices  59.3 us (31%)
  Pallas kernels  32.2 us (17%)
  waiting for transfers between devices  31.9 us (17%)
  local copies, waits for them, and re-layouts  2.33 us (1%)
    ppermute x3, starting transfers between devices, swap_halves(): return lax.ppermute(x, 'half', [(0, 1), (1, 0)])  41.6 us
    all_to_all x2, blocking collectives, plane_gather(): lax.all_to_all(jnp.broadcast_to(part[None], (size, *part.shape)), PLANE,...  40.7 us
    pallas_call x6, Pallas kernels, kernel_call(): pl.pallas_call(body, out_shape=[jax.ShapeDtypeStruct(shape, jnp.float32)...  31.1 us
    all_to_all x1, blocking collectives, plane_scatter(): return lax.all_to_all(parts, PLANE, 0, 0, tiled=True).sum(axis=0)  21.3 us
    ppermute x4, waiting for transfers between devices, line_total(): x = x + lax.ppermute(x, 'zh', [(i, i ^ step) for i in range(size)])  17.6 us
    all_to_all x1, waiting for transfers between devices, plane_scatter(): return lax.all_to_all(parts, PLANE, 0, 0, tiled=True).sum(axis=0)  13.5 us
    all_to_all x1, starting transfers between devices, plane_scatter(): return lax.all_to_all(parts, PLANE, 0, 0, tiled=True).sum(axis=0)  9.49 us
    ppermute x4, starting transfers between devices, line_total(): x = x + lax.ppermute(x, 'zh', [(i, i ^ step) for i in range(size)])  4.39 us
  transfers between devices with their start and end apart: 12, of which 6 were waited for; matrix products, arithmetic and copies ran while one was open for 1% of the time, Pallas kernels for 11%

profile of v1, /device:TPU:1, one launch (start us, length us, event | category | flops | bytes accessed | tf_op | source)
XLA Modules:
  0.0 190.0 jit_solution(7265625771932561771)
XLA Ops:
  0.6 0.7 collective-permute-start
  1.4 0.9 copy.7.density_ref
  2.3 0.1 pad_add_fusion.meta
  2.4 0.0 copy-start
  2.4 1.2 copy-done
  3.6 3.9 %shard_map.50.refs_2_ = f32[1024,256]{1,0:T(8,128)} custom-call(s32[2]{0:T(128)S(1)} %pad_add_fusion.meta, f32[1024,256]{1,0:T(8,128)S(1)} %bitcast.10, f32[1024,1]{1,0:T(8,128)S(1)} %copy.7.density_ref), custom_call_target="tpu_custom_call" | custom-call | tf_op jit(solution)/shard_map/pallas_call | solution.py:87
  7.5 0.0 collective-permute-done.refs_1_.previous_ref
  7.6 0.6 across.2
  8.1 0.0 copy-start.1
  8.1 9.5 %all-to-all-start = ((f32[32,32,256]{2,1,0:T(8,128)}), f32[32,32,256]{2,1,0:T(8,128)}, u32[]{:S(2)}, u32[]{:S(2)}) async-start(f32[32,32,256]{2,1,0:T(8,128)} %bitcast.4), calls=%async_computation | async-start | bytes 2097152 | tf_op jit(solution)/shard_map/all_to_all | solution.py:52
  17.6 0.0 copy-done.1
  17.6 1.7 collective-permute-start.4
  19.3 13.5 %all-to-all-done = f32[32,32,256]{2,1,0:T(8,128)} async-done(((f32[32,32,256]{2,1,0:T(8,128)}), f32[32,32,256]{2,1,0:T(8,128)}, u32[]{:S(2)}, u32[]{:S(2)}) %all-to-all-start) | async-done | bytes 1048608 | tf_op jit(solution)/shard_map/all_to_all | solution.py:52
  32.8 1.3 reduce_sum.18
  34.1 0.4 collective-permute-start.1
  34.5 3.3 %collective-permute-done.1 = f32[32,256]{1,0:T(8,128)S(1)} collective-permute-done((f32[32,256]{1,0:T(8,128)S(1)}, f32[32,256]{1,0:T(8,128)S(1)}, u32[]{:S(2)}, u32[]{:S(2)}) %collective-permute-start.1) | collective-permute-done | bytes 32800 | tf_op jit(solution)/shard_map/ppermute | solution.py:67
  37.8 3.9 %collective-permute-start.2 = (f32[32,256]{1,0:T(8,128)S(1)}, f32[32,256]{1,0:T(8,128)S(1)}, u32[]{:S(2)}, u32[]{:S(2)}) collective-permute-start(f32[32,256]{1,0:T(8,128)S(1)} %add.24), channel_id=1, source_target_pairs={{0,4},{2,6},{4,0},{6,2},{1,5},{3,7},{5,1},{7,3},{8,12},{10,14},{12... | collective-permute-start | bytes 98312 | tf_op jit(solution)/shard_map/ppermute | solution.py:67
  41.7 3.2 %collective-permute-done.2 = f32[32,256]{1,0:T(8,128)S(1)} collective-permute-done((f32[32,256]{1,0:T(8,128)S(1)}, f32[32,256]{1,0:T(8,128)S(1)}, u32[]{:S(2)}, u32[]{:S(2)}) %collective-permute-start.2) | collective-permute-done | bytes 32800 | tf_op jit(solution)/shard_map/ppermute | solution.py:67
  44.9 20.9 %collective-permute-start.3 = (f32[32,256]{1,0:T(8,128)S(1)}, f32[32,256]{1,0:T(8,128)S(1)}, u32[]{:S(2)}, u32[]{:S(2)}) collective-permute-start(f32[32,256]{1,0:T(8,128)S(1)} %add.25), channel_id=1, source_target_pairs={{0,128},{128,0},{1,129},{129,1},{2,130},{130,2},{3,131},{131,3},{4... | collective-permute-start | bytes 98312 | tf_op jit(solution)/shard_map/ppermute | solution.py:73
  65.8 0.0 collective-permute-done.4.following_ref
  65.8 0.9 collective-permute-done.3
  66.6 0.1 broadcast_in_dim.9
  66.8 0.0 copy-start.2
  66.8 21.9 %all_to_all.20 = f32[32,32,256]{2,1,0:T(8,128)S(1)} all-to-all(f32[32,32,256]{2,1,0:T(8,128)S(1)} %broadcast_in_dim.9), channel_id=1, replica_groups=mesh['half'=2,'y'=4,'x'=4,'zh'=4,'zl'=2] {'y','x','zl'}, dimensions={0} | all-to-all | bytes 2097152 | tf_op jit(solution)/shard_map/all_to_all | solution.py:57
  88.7 0.0 copy-done.2
  88.7 4.5 %shard_map.51 = (f32[512,256]{1,0:T(8,128)S(1)}, f32[512,256]{1,0:T(8,128)S(1)}) custom-call(s32[2]{0:T(128)S(1)} %pad_add_fusion.meta, f32[1024,256]{1,0:T(8,128)S(1)} %bitcast.13, f32[1024,256]{1,0:T(8,128)} %collective-permute-done.4.following_ref, f32[1024,256]{1,0:T(8,128)S(1)} %collective-permute-done.refs_1_.previous_ref, f32[1024,256]{1,0:T(8,128)S(1)} %bitcast.19, ...), custom_call_target="tpu_custom_call" | custom-call | tf_op jit(solution)/shard_map/pallas_call | solution.py:87
  93.2 0.7 collective-permute-start.5
  93.9 0.7 collective-permute-start.6
  94.6 4.0 %shard_map.52 = (f32[1280,256]{1,0:T(8,128)S(1)}, f32[1024,256]{1,0:T(8,128)S(1)}) custom-call(s32[2]{0:T(128)S(1)} %pad_add_fusion.meta, f32[512,256]{1,0:T(8,128)S(1)} %get-tuple-element.10.low_ref.refs_0_, f32[512,256]{1,0:T(8,128)S(1)} %get-tuple-element.11.high_ref.refs_1_, f32[1024,256]{1,0:T(8,128)S(1)} %bitcast.14, f32[1024,1]{1,0:T(8,128)S(1)} %copy.7.density_ref), custom_call_target="tpu_custom_call" | custom-call | tf_op jit(solution)/shard_map/pallas_call | solution.py:87
  98.6 0.0 collective-permute-done.5.refs_2_
  98.6 0.0 collective-permute-done.6.refs_3_
  98.6 0.6 across.3
  99.2 21.3 %all_to_all.21 = f32[32,40,256]{2,1,0:T(8,128)S(1)} all-to-all(f32[32,40,256]{2,1,0:T(8,128)S(1)} %bitcast.18), channel_id=1, replica_groups=mesh['half'=2,'y'=4,'x'=4,'zh'=4,'zl'=2] {'y','x','zl'}, dimensions={0} | all-to-all | bytes 2621440 | tf_op jit(solution)/shard_map/all_to_all | solution.py:52
  120.5 0.1 reduce_sum.19
  120.5 0.1 collective-permute-start.7
  120.6 3.7 %collective-permute-done.7 = f32[40,256]{1,0:T(8,128)S(1)} collective-permute-done((f32[40,256]{1,0:T(8,128)S(1)}, f32[40,256]{1,0:T(8,128)S(1)}, u32[]{:S(2)}, u32[]{:S(2)}) %collective-permute-start.7) | collective-permute-done | bytes 40992 | tf_op jit(solution)/shard_map/ppermute | solution.py:67
  124.4 0.0 collective-permute-start.8
  124.4 7.3 %collective-permute-done.8 = f32[40,256]{1,0:T(8,128)S(1)} collective-permute-done((f32[40,256]{1,0:T(8,128)S(1)}, f32[40,256]{1,0:T(8,128)S(1)}, u32[]{:S(2)}, u32[]{:S(2)}) %collective-permute-start.8) | collective-permute-done | bytes 40992 | tf_op jit(solution)/shard_map/ppermute | solution.py:67
  131.7 0.1 broadcast_in_dim.20
  131.8 18.8 %all_to_all.22 = f32[32,40,256]{2,1,0:T(8,128)S(1)} all-to-all(f32[32,40,256]{2,1,0:T(8,128)S(1)} %broadcast_in_dim.20), channel_id=1, replica_groups=mesh['half'=2,'y'=4,'x'=4,'zh'=4,'zl'=2] {'y','x','zl'}, dimensions={0} | all-to-all | bytes 2621440 | tf_op jit(solution)/shard_map/all_to_all | solution.py:57
  150.6 20.6 %collective-permute-start.9 = (f32[1280,256]{1,0:T(8,128)S(1)}, f32[1280,256]{1,0:T(8,128)S(1)}, u32[]{:S(2)}, u32[]{:S(2)}) collective-permute-start(f32[1280,256]{1,0:T(8,128)S(1)} %bitcast.15), channel_id=1, source_target_pairs={{0,128},{128,0},{1,129},{129,1},{2,130},{130,2},{3,131},{131,3},{4... | collective-permute-start | bytes 3932168 | tf_op jit(solution)/shard_map/ppermute | solution.py:73
  171.2 10.2 %shard_map.53.inverse_ref = f32[256,256]{1,0:T(8,128)S(1)} custom-call(s32[2]{0:T(128)S(1)} %pad_add_fusion.meta, f32[1280,256]{1,0:T(8,128)S(1)} %bitcast.16), custom_call_target="tpu_custom_call" | custom-call | tf_op jit(solution)/shard_map/pallas_call | solution.py:87
  181.4 0.1 collective-permute-start.10
  181.5 2.5 %shard_map.54 = f32[1024,256]{1,0:T(8,128)} custom-call(s32[2]{0:T(128)S(1)} %pad_add_fusion.meta, f32[1024,256]{1,0:T(8,128)S(1)} %get-tuple-element.12.k_ref, f32[256,256]{1,0:T(8,128)S(1)} %shard_map.53.inverse_ref), custom_call_target="tpu_custom_call" | custom-call | tf_op jit(solution)/shard_map/pallas_call | solution.py:87
  184.1 0.0 collective-permute-done.10.other_inverse_ref
  184.1 0.0 collective-permute-done.9.other_ref
  184.1 5.9 %shard_map.55 = f32[128,256]{1,0:T(8,128)} custom-call(s32[2]{0:T(128)S(1)} %pad_add_fusion.meta, f32[1280,256]{1,0:T(8,128)S(1)} %bitcast.17, f32[1280,256]{1,0:T(8,128)S(1)} %collective-permute-done.9.other_ref, f32[256,256]{1,0:T(8,128)S(1)} %shard_map.53.inverse_ref, f32[256,256]{1,0:T(8,128)S(1)} %collective-permute-done.10.other_inverse_ref, ...), custom_call_target="tpu_custom_call" | custom-call | tf_op jit(solution)/shard_map/pallas_call | solution.py:87
  (4 shorter events, 0.0 us)
Async XLA Ops:
  0.6 6.9 %collective-permute-start = (f32[1024,256]{1,0:T(8,128)}, f32[1024,256]{1,0:T(8,128)S(1)}, u32[]{:S(2)}, u32[]{:S(2)}) collective-permute-start(f32[1024,256]{1,0:T(8,128)} %bitcast.9), channel_id=1, source_target_pairs={{0,1},{1,2},{2,3},{3,4},{4,5},{5,6},{6,7},{7,8},{8,9},{9,10},{10,1... | collective-permute-start | bytes 3145736 | tf_op jit(solution)/shard_map/ppermute | solution.py:78
  2.4 1.2 copy-start
  8.1 9.5 %copy-start.1 = (f32[1,1024,256]{2,1,0:T(8,128)S(1)}, f32[1,1024,256]{2,1,0:T(8,128)}, u32[]{:S(2)}) copy-start(f32[1,1024,256]{2,1,0:T(8,128)} %param.3) | copy-start | bytes 3145732
  8.1 24.6 %all-to-all-start = ((f32[32,32,256]{2,1,0:T(8,128)}), f32[32,32,256]{2,1,0:T(8,128)}, u32[]{:S(2)}, u32[]{:S(2)}) async-start(f32[32,32,256]{2,1,0:T(8,128)} %bitcast.4), calls=%async_computation | async-start | bytes 2097152 | tf_op jit(solution)/shard_map/all_to_all | solution.py:52
  17.6 48.2 %collective-permute-start.4 = (f32[1024,256]{1,0:T(8,128)S(1)}, f32[1024,256]{1,0:T(8,128)}, u32[]{:S(2)}, u32[]{:S(2)}) collective-permute-start(f32[1024,256]{1,0:T(8,128)S(1)} %bitcast.12), channel_id=1, source_target_pairs={{0,127},{1,0},{2,1},{3,2},{4,3},{5,4},{6,5},{7,6},{8,7},{9,8},{10,... | collective-permute-start | bytes 3145736 | tf_op jit(solution)/shard_map/ppermute | solution.py:78
  34.1 3.8 %collective-permute-start.1 = (f32[32,256]{1,0:T(8,128)S(1)}, f32[32,256]{1,0:T(8,128)S(1)}, u32[]{:S(2)}, u32[]{:S(2)}) collective-permute-start(f32[32,256]{1,0:T(8,128)S(1)} %reduce_sum.18), channel_id=1, source_target_pairs={{0,2},{2,0},{4,6},{6,4},{1,3},{3,1},{5,7},{7,5},{8,10},{10,8},{12,... | collective-permute-start | bytes 98312 | tf_op jit(solution)/shard_map/ppermute | solution.py:67
  37.8 7.1 %collective-permute-start.2 = (f32[32,256]{1,0:T(8,128)S(1)}, f32[32,256]{1,0:T(8,128)S(1)}, u32[]{:S(2)}, u32[]{:S(2)}) collective-permute-start(f32[32,256]{1,0:T(8,128)S(1)} %add.24), channel_id=1, source_target_pairs={{0,4},{2,6},{4,0},{6,2},{1,5},{3,7},{5,1},{7,3},{8,12},{10,14},{12... | collective-permute-start | bytes 98312 | tf_op jit(solution)/shard_map/ppermute | solution.py:67
  44.9 21.7 %collective-permute-start.3 = (f32[32,256]{1,0:T(8,128)S(1)}, f32[32,256]{1,0:T(8,128)S(1)}, u32[]{:S(2)}, u32[]{:S(2)}) collective-permute-start(f32[32,256]{1,0:T(8,128)S(1)} %add.25), channel_id=1, source_target_pairs={{0,128},{128,0},{1,129},{129,1},{2,130},{130,2},{3,131},{131,3},{4... | collective-permute-start | bytes 98312 | tf_op jit(solution)/shard_map/ppermute | solution.py:73
  66.8 21.9 %copy-start.2 = (f32[256,256]{1,0:T(8,128)S(1)}, f32[256,256]{1,0:T(8,128)}, u32[]{:S(2)}) copy-start(f32[256,256]{1,0:T(8,128)} %s_ref.3) | copy-start | bytes 786436
  93.2 5.4 %collective-permute-start.5 = (f32[512,256]{1,0:T(8,128)S(1)}, f32[512,256]{1,0:T(8,128)S(1)}, u32[]{:S(2)}, u32[]{:S(2)}) collective-permute-start(f32[512,256]{1,0:T(8,128)S(1)} %get-tuple-element.10.low_ref.refs_0_), channel_id=1, source_target_pairs={{0,127},{1,0},{2,1},{3,2},{4,3},{5,4},{6,5},{7,6},{8,7},{9,8},{10,... | collective-permute-start | bytes 1572872 | tf_op jit(solution)/shard_map/ppermute | solution.py:78
  93.9 4.7 %collective-permute-start.6 = (f32[512,256]{1,0:T(8,128)S(1)}, f32[512,256]{1,0:T(8,128)S(1)}, u32[]{:S(2)}, u32[]{:S(2)}) collective-permute-start(f32[512,256]{1,0:T(8,128)S(1)} %get-tuple-element.11.high_ref.refs_1_), channel_id=1, source_target_pairs={{0,1},{1,2},{2,3},{3,4},{4,5},{5,6},{6,7},{7,8},{8,9},{9,10},{10,1... | collective-permute-start | bytes 1572872 | tf_op jit(solution)/shard_map/ppermute | solution.py:78
  120.5 3.8 %collective-permute-start.7 = (f32[40,256]{1,0:T(8,128)S(1)}, f32[40,256]{1,0:T(8,128)S(1)}, u32[]{:S(2)}, u32[]{:S(2)}) collective-permute-start(f32[40,256]{1,0:T(8,128)S(1)} %reduce_sum.19), channel_id=1, source_target_pairs={{0,2},{2,0},{4,6},{6,4},{1,3},{3,1},{5,7},{7,5},{8,10},{10,8},{12,... | collective-permute-start | bytes 122888 | tf_op jit(solution)/shard_map/ppermute | solution.py:67
  124.4 7.3 %collective-permute-start.8 = (f32[40,256]{1,0:T(8,128)S(1)}, f32[40,256]{1,0:T(8,128)S(1)}, u32[]{:S(2)}, u32[]{:S(2)}) collective-permute-start(f32[40,256]{1,0:T(8,128)S(1)} %add.26), channel_id=1, source_target_pairs={{0,4},{2,6},{4,0},{6,2},{1,5},{3,7},{5,1},{7,3},{8,12},{10,14},{12... | collective-permute-start | bytes 122888 | tf_op jit(solution)/shard_map/ppermute | solution.py:67
  150.6 33.5 %collective-permute-start.9 = (f32[1280,256]{1,0:T(8,128)S(1)}, f32[1280,256]{1,0:T(8,128)S(1)}, u32[]{:S(2)}, u32[]{:S(2)}) collective-permute-start(f32[1280,256]{1,0:T(8,128)S(1)} %bitcast.15), channel_id=1, source_target_pairs={{0,128},{128,0},{1,129},{129,1},{2,130},{130,2},{3,131},{131,3},{4... | collective-permute-start | bytes 3932168 | tf_op jit(solution)/shard_map/ppermute | solution.py:73
  181.4 2.6 %collective-permute-start.10 = (f32[256,256]{1,0:T(8,128)S(1)}, f32[256,256]{1,0:T(8,128)S(1)}, u32[]{:S(2)}, u32[]{:S(2)}) collective-permute-start(f32[256,256]{1,0:T(8,128)S(1)} %shard_map.53.inverse_ref), channel_id=1, source_target_pairs={{0,128},{128,0},{1,129},{129,1},{2,130},{130,2},{3,131},{131,3},{4... | collective-permute-start | bytes 786440 | tf_op jit(solution)/shard_map/ppermute | solution.py:73
